TPU v7x, 32 devices: a whole 2x2x4 slice. The times are simulated.
32 devices in a mesh: shard: 2 (over y), ctx: 4 (over x, core), tp: 4 (over z).
Axes of the slice: x: 2, y: 2, z: 4, core: 2. Of those that a mesh axis runs over, the one named last changes fastest.
Arguments:
- video: bfloat16 [2, 16, 16, 16, 1152], P('shard', 'ctx', 'tp'), may hold values from -6 to 6
- cond: bfloat16 [2, 1152], P('shard'), may hold values from -6 to 6
- w_ada: bfloat16 [2, 1152, 6912], P(None, 'shard', 'tp'), may hold values from -0.1875 to 0.1875
- b_ada: bfloat16 [2, 6912], P(None, 'tp'), may hold values from 0.5 to 1.5
- w_qkv: bfloat16 [2, 3, 1152, 1152], P(None, None, 'shard', 'tp'), may hold values from -0.09375 to 0.09375
- b_qv: bfloat16 [2, 2, 1152], P(None, None, 'tp'), may hold values from -3 to 3
- w_out: bfloat16 [2, 1152, 1152], P(None, 'tp', 'shard'), may hold values from -0.75 to 0.75
- b_out: bfloat16 [2, 1152], replicated, may hold values from -3 to 3
- w_up: bfloat16 [2, 1152, 4608], P(None, 'shard', 'tp'), may hold values from -0.09375 to 0.09375
- b_up: bfloat16 [2, 4608], P(None, 'tp'), may hold values from -3 to 3
- w_down: bfloat16 [2, 4608, 1152], P(None, 'tp', 'shard'), may hold values from -0.09375 to 0.09375
- b_down: bfloat16 [2, 1152], replicated, may hold values from -3 to 3
- cotangent: bfloat16 [2, 16, 16, 16, 1152], P('shard', None, 'tp', 'ctx'), may hold values from -6 to 6
Outputs:
- out: bfloat16 [2, 16, 16, 16, 1152], P('shard', None, 'tp', 'ctx')
- grad_video: float32 [2, 16, 16, 16, 1152], P('shard', 'ctx', 'tp')
- grad_cond: float32 [2, 1152], P('shard')
- grad_w_ada: float32 [2, 1152, 6912], P(None, 'shard', 'tp')
- grad_b_ada: float32 [2, 6912], P(None, 'tp')
- grad_w_qkv: float32 [2, 3, 1152, 1152], P(None, None, 'shard', 'tp')
- grad_b_qv: float32 [2, 2, 1152], P(None, None, 'tp')
- grad_w_out: float32 [2, 1152, 1152], P(None, 'tp', 'shard')
- grad_b_out: float32 [2, 1152], replicated
- grad_w_up: float32 [2, 1152, 4608], P(None, 'shard', 'tp')
- grad_b_up: float32 [2, 4608], P(None, 'tp')
- grad_w_down: float32 [2, 4608, 1152], P(None, 'tp', 'shard')
- grad_b_down: float32 [2, 1152], replicated
All inputs are finite; a program needn't handle non-finite values.
Results may differ from a plain program's by a relative error of at most 0.025.
Values may be sent and summed in bfloat16 or wider, within the bound.
No kernel may reach another device: no remote copies, remote signals or barrier semaphores. Data moves between devices by JAX's collectives and lax.ppermute only.
A program may use at most 256 MiB of HBM per device.

v0:
```python
from functools import partial
import math

import jax
import jax.numpy as jnp
from jax import lax
from jax.sharding import PartitionSpec as P

HEAD_DIM = 72


highest = lax.Precision.HIGHEST


def layer_norm(values):
    average = jnp.mean(values, axis=-1, keepdims=True)
    centered = values - average
    spread = jnp.mean(centered * centered, axis=-1, keepdims=True)
    return centered * lax.rsqrt(spread + 1e-06)


def modulate(values, offset, factor):
    return layer_norm(values) * (1.0 + factor) + offset


def split_mod(modulation):
    pieces = modulation.reshape(modulation.shape[0], 6, 1, 1, 1, modulation.shape[1] // 6)
    return [pieces[:, number] for number in range(6)]


def to_sequences(rows, grid, temporal):
    heads = rows.reshape(grid + (-1, HEAD_DIM))
    head_count = heads.shape[5]
    if temporal:
        heads = jnp.transpose(heads, (0, 1, 3, 4, 2, 5, 6))
        return heads.reshape(-1, grid[2], head_count, HEAD_DIM)
    heads = jnp.transpose(heads, (1, 2, 0, 3, 4, 5, 6))
    return heads.reshape(grid[1] * grid[2], -1, head_count, HEAD_DIM)


def from_sequences(heads, grid, temporal):
    head_count = heads.shape[2]
    if temporal:
        heads = heads.reshape(grid[0], grid[1], grid[3], grid[4], grid[2], head_count, HEAD_DIM)
        heads = jnp.transpose(heads, (0, 1, 4, 2, 3, 5, 6))
    else:
        heads = heads.reshape(grid[1], grid[2], grid[0], grid[3], grid[4], head_count, HEAD_DIM)
        heads = jnp.transpose(heads, (2, 0, 1, 3, 4, 5, 6))
    return heads.reshape(-1, head_count * HEAD_DIM)


def attend(query_seq, key_seq, value_seq):
    factor = 1.0 / math.sqrt(HEAD_DIM)
    scores = (
        jnp.einsum("bqhe,bkhe->bhqk", query_seq, key_seq, preferred_element_type=jnp.float32)
        * factor
    )
    row_max = jnp.max(scores, axis=-1, keepdims=True)
    weights = jnp.exp(scores - row_max)
    totals = jnp.sum(weights, axis=-1, keepdims=True)
    probs_low = (weights / totals).astype(jnp.bfloat16)
    attended = jnp.einsum(
        "bhqk,bkhe->bqhe", probs_low, value_seq, preferred_element_type=jnp.float32
    )
    return (attended.astype(jnp.bfloat16), row_max + jnp.log(totals))


def attend_back(query_seq, key_seq, value_seq, log_total, grad_out):
    factor = 1.0 / math.sqrt(HEAD_DIM)
    scores = (
        jnp.einsum("bqhe,bkhe->bhqk", query_seq, key_seq, preferred_element_type=jnp.float32)
        * factor
    )
    probs = jnp.exp(scores - log_total)
    grad_value = jnp.einsum(
        "bhqk,bqhe->bkhe", probs.astype(jnp.bfloat16), grad_out, preferred_element_type=jnp.float32
    ).astype(jnp.bfloat16)
    grad_probs = jnp.einsum(
        "bqhe,bkhe->bhqk", grad_out, value_seq, preferred_element_type=jnp.float32
    )
    inner = jnp.sum(grad_probs * probs, axis=-1, keepdims=True)
    grad_scores = (probs * (grad_probs - inner)).astype(jnp.bfloat16)
    grad_query = (
        jnp.einsum("bhqk,bkhe->bqhe", grad_scores, key_seq, preferred_element_type=jnp.float32)
        * factor
    ).astype(jnp.bfloat16)
    grad_key = (
        jnp.einsum("bhqk,bqhe->bkhe", grad_scores, query_seq, preferred_element_type=jnp.float32)
        * factor
    ).astype(jnp.bfloat16)
    return (grad_query, grad_key, grad_value)


def fetch_forward(number, w_ada, w_qkv, w_out, w_up, w_down):
    return (
        lax.all_gather(w_ada[number], "shard", axis=0, tiled=True),
        lax.all_gather(w_qkv[number], "shard", axis=1, tiled=True),
        lax.all_gather(w_out[number], "shard", axis=1, tiled=True),
        lax.all_gather(w_up[number], "shard", axis=0, tiled=True),
        lax.all_gather(w_down[number], "shard", axis=1, tiled=True),
    )


def fetch_again(number, w_ada, w_qkv, w_out, w_up, w_down):
    return (
        lax.all_gather(w_ada[number], "shard", axis=0, tiled=True),
        lax.all_gather(w_qkv[number], "shard", axis=1, tiled=True),
        lax.all_gather(w_out[number], "shard", axis=1, tiled=True),
        lax.all_gather(w_up[number], "shard", axis=0, tiled=True),
        lax.all_gather(w_down[number], "shard", axis=1, tiled=True),
    )


def spread_rows(values):
    return lax.all_gather(values[None], "tp", axis=0, tiled=True)


def spread_grads(values):
    return lax.all_gather(values[None], "tp", axis=0, tiled=True)


def reduce_rows(term, own_rows):
    return lax.psum_scatter(
        term(jnp.int32(0), own_rows * lax.axis_size("tp")), "tp", scatter_dimension=0, tiled=True
    )


def reduce_grads(term, own_rows):
    return lax.psum_scatter(
        term(jnp.int32(0), own_rows * lax.axis_size("tp")), "tp", scatter_dimension=0, tiled=True
    )


def sum_weight_grads(grads):
    summed = (
        lax.psum_scatter(
            grads[0].astype(jnp.bfloat16), "shard", scatter_dimension=0, tiled=True
        ).astype(jnp.float32),
        lax.psum_scatter(
            grads[1].astype(jnp.bfloat16), "shard", scatter_dimension=1, tiled=True
        ).astype(jnp.float32),
        lax.psum_scatter(
            grads[2].astype(jnp.bfloat16), "shard", scatter_dimension=1, tiled=True
        ).astype(jnp.float32),
        lax.psum_scatter(
            grads[3].astype(jnp.bfloat16), "shard", scatter_dimension=0, tiled=True
        ).astype(jnp.float32),
        lax.psum_scatter(
            grads[4].astype(jnp.bfloat16), "shard", scatter_dimension=1, tiled=True
        ).astype(jnp.float32),
    )
    return (
        lax.psum(summed[0].astype(jnp.bfloat16), "ctx").astype(jnp.float32),
        lax.psum(summed[1].astype(jnp.bfloat16), "ctx").astype(jnp.float32),
        lax.psum(summed[2].astype(jnp.bfloat16), "ctx").astype(jnp.float32),
        lax.psum(summed[3].astype(jnp.bfloat16), "ctx").astype(jnp.float32),
        lax.psum(summed[4].astype(jnp.bfloat16), "ctx").astype(jnp.float32),
    )


def row_product(left, right, first_row, row_count):
    return jnp.dot(left, right, preferred_element_type=jnp.float32)


def row_product_back(left, right, first_row, row_count):
    return jnp.einsum("rf,df->rd", left, right, preferred_element_type=jnp.float32)


def qkv_product_back(left, right, first_row, row_count):
    return jnp.einsum("trc,tdc->rd", left, right, preferred_element_type=jnp.float32)


def forward_block(inputs, cond_act, gathered, b_ada, b_qv, b_out, b_up, b_down, temporal):
    ada_full, qkv_full, out_full, up_full, down_full = gathered
    width = inputs.shape[-1]
    own_rows = inputs.shape[0] * inputs.shape[1] * inputs.shape[2] * inputs.shape[3]
    mod_part = jnp.dot(cond_act, ada_full, preferred_element_type=jnp.float32) + b_ada
    modulation = lax.all_gather(mod_part, "tp", axis=1, tiled=True)
    shift_a, scale_a, gate_a, shift_m, scale_m, gate_m = split_mod(modulation)
    hidden = spread_rows(modulate(inputs, shift_a, scale_a).astype(jnp.bfloat16))
    grid = hidden.shape[:5]
    hidden_rows = hidden.reshape(-1, width)
    projected = jnp.einsum("rd,tdc->trc", hidden_rows, qkv_full, preferred_element_type=jnp.float32)
    query_seq = to_sequences((projected[0] + b_qv[0]).astype(jnp.bfloat16), grid, temporal)
    key_seq = to_sequences(projected[1].astype(jnp.bfloat16), grid, temporal)
    value_seq = to_sequences((projected[2] + b_qv[1]).astype(jnp.bfloat16), grid, temporal)
    attended, log_total = attend(query_seq, key_seq, value_seq)
    attended_rows = from_sequences(attended, grid, temporal)
    attn_out = (
        reduce_rows(partial(row_product, attended_rows, out_full), own_rows) + b_out
    ).reshape(inputs.shape)
    after_attn = inputs + gate_a * attn_out
    hidden_two = spread_rows(modulate(after_attn, shift_m, scale_m).astype(jnp.bfloat16)).reshape(
        -1, width
    )
    up_rows = jnp.dot(hidden_two, up_full, preferred_element_type=jnp.float32) + b_up
    activated = jax.nn.gelu(up_rows, approximate=True).astype(jnp.bfloat16)
    mlp_out = (reduce_rows(partial(row_product, activated, down_full), own_rows) + b_down).reshape(
        inputs.shape
    )
    result = after_attn + gate_m * mlp_out
    kept = (
        inputs,
        after_attn,
        modulation,
        hidden_rows,
        query_seq,
        key_seq,
        value_seq,
        log_total,
        attended_rows,
        attn_out,
        hidden_two,
        up_rows,
        mlp_out,
        grid,
    )
    return (result, kept)


def backward_block(grad_y, kept, gathered, cond_act, temporal):
    (
        inputs,
        after_attn,
        modulation,
        hidden_rows,
        query_seq,
        key_seq,
        value_seq,
        log_total,
        attended_rows,
        attn_out,
        hidden_two,
        up_rows,
        mlp_out,
        grid,
    ) = kept
    ada_full, qkv_full, out_full, up_full, down_full = gathered
    width = inputs.shape[-1]
    clips = inputs.shape[0]
    own_rows = inputs.shape[0] * inputs.shape[1] * inputs.shape[2] * inputs.shape[3]
    shift_a, scale_a, gate_a, shift_m, scale_m, gate_m = split_mod(modulation)
    token_axes = (1, 2, 3)
    grad_mlp = (gate_m * grad_y).astype(jnp.bfloat16)
    grad_gate_m = jnp.sum(grad_y * mlp_out, axis=token_axes)
    grad_mlp_rows = spread_grads(grad_mlp).reshape(-1, width)
    grad_b_down = jnp.sum(grad_mlp_rows, axis=0, dtype=jnp.float32)
    activated, gelu_back = jax.vjp(partial(jax.nn.gelu, approximate=True), up_rows)
    grad_w_down = jnp.einsum(
        "rf,rd->fd",
        activated.astype(jnp.bfloat16),
        grad_mlp_rows,
        preferred_element_type=jnp.float32,
    )
    grad_act = jnp.einsum("rd,fd->rf", grad_mlp_rows, down_full, preferred_element_type=jnp.float32)
    grad_up = gelu_back(grad_act)[0].astype(jnp.bfloat16)
    grad_b_up = jnp.sum(grad_up, axis=0, dtype=jnp.float32)
    grad_w_up = jnp.einsum("rd,rf->df", hidden_two, grad_up, preferred_element_type=jnp.float32)
    grad_hidden_two = reduce_grads(partial(row_product_back, grad_up, up_full), own_rows).reshape(
        inputs.shape
    )
    unused_two, norm_back_two = jax.vjp(modulate, after_attn, shift_m, scale_m)
    grad_norm_two, grad_shift_m, grad_scale_m = norm_back_two(grad_hidden_two)
    grad_after = grad_y + grad_norm_two
    grad_attn = (gate_a * grad_after).astype(jnp.bfloat16)
    grad_gate_a = jnp.sum(grad_after * attn_out, axis=token_axes)
    grad_attn_rows = spread_grads(grad_attn).reshape(-1, width)
    grad_b_out = jnp.sum(grad_attn_rows, axis=0, dtype=jnp.float32)
    grad_w_out = jnp.einsum(
        "rc,rd->cd", attended_rows, grad_attn_rows, preferred_element_type=jnp.float32
    )
    grad_attended = jnp.einsum(
        "rd,cd->rc", grad_attn_rows, out_full, preferred_element_type=jnp.float32
    ).astype(jnp.bfloat16)
    grad_query, grad_key, grad_value = attend_back(
        query_seq, key_seq, value_seq, log_total, to_sequences(grad_attended, grid, temporal)
    )
    grad_proj = jnp.stack(
        [
            from_sequences(grad_query, grid, temporal),
            from_sequences(grad_key, grid, temporal),
            from_sequences(grad_value, grid, temporal),
        ]
    )
    grad_b_qv = jnp.stack(
        [
            jnp.sum(grad_proj[0], axis=0, dtype=jnp.float32),
            jnp.sum(grad_proj[2], axis=0, dtype=jnp.float32),
        ]
    )
    grad_w_qkv = jnp.einsum(
        "rd,trc->tdc", hidden_rows, grad_proj, preferred_element_type=jnp.float32
    )
    grad_hidden = reduce_grads(partial(qkv_product_back, grad_proj, qkv_full), own_rows).reshape(
        inputs.shape
    )
    unused_one, norm_back_one = jax.vjp(modulate, inputs, shift_a, scale_a)
    grad_norm_one, grad_shift_a, grad_scale_a = norm_back_one(grad_hidden)
    grad_inputs = grad_after + grad_norm_one
    grad_mod = jnp.concatenate(
        [
            grad_shift_a.reshape(clips, width),
            grad_scale_a.reshape(clips, width),
            grad_gate_a,
            grad_shift_m.reshape(clips, width),
            grad_scale_m.reshape(clips, width),
            grad_gate_m,
        ],
        axis=1,
    )
    grad_mod_part = lax.psum_scatter(grad_mod, "tp", scatter_dimension=1, tiled=True)
    grad_w_ada = jnp.dot(cond_act.astype(jnp.float32).T, grad_mod_part, precision=highest)
    grad_b_ada = jnp.sum(grad_mod_part, axis=0)
    grad_cond_part = jnp.dot(grad_mod_part, ada_full.astype(jnp.float32).T, precision=highest)
    summed = sum_weight_grads((grad_w_ada, grad_w_qkv, grad_w_out, grad_w_up, grad_w_down))
    biases = (grad_b_ada, grad_b_qv, grad_b_out, grad_b_up, grad_b_down)
    return (grad_inputs, summed, biases, grad_cond_part)


def body(
    video, cond, w_ada, b_ada, w_qkv, b_qv, w_out, b_out, w_up, b_up, w_down, b_down, cotangent
):
    cond_float = cond.astype(jnp.float32)
    silu_value, silu_back = jax.vjp(jax.nn.silu, cond_float)
    cond_act = silu_value.astype(jnp.bfloat16)
    first = fetch_forward(0, w_ada, w_qkv, w_out, w_up, w_down)
    middle, kept_one = forward_block(
        video.astype(jnp.float32),
        cond_act,
        first,
        b_ada[0],
        b_qv[0],
        b_out[0],
        b_up[0],
        b_down[0],
        False,
    )
    moved = lax.all_to_all(
        middle.astype(jnp.bfloat16), "ctx", split_axis=3, concat_axis=1, tiled=True
    )
    second = fetch_forward(1, w_ada, w_qkv, w_out, w_up, w_down)
    result, kept_two = forward_block(
        moved.astype(jnp.float32),
        cond_act,
        second,
        b_ada[1],
        b_qv[1],
        b_out[1],
        b_up[1],
        b_down[1],
        True,
    )
    second_back = fetch_again(1, w_ada, w_qkv, w_out, w_up, w_down)
    grad_moved, grads_two, biases_two, cond_two = backward_block(
        cotangent.astype(jnp.float32), kept_two, second_back, cond_act, True
    )
    grad_middle = lax.all_to_all(
        grad_moved.astype(jnp.bfloat16), "ctx", split_axis=1, concat_axis=3, tiled=True
    ).astype(jnp.float32)
    first_back = fetch_again(0, w_ada, w_qkv, w_out, w_up, w_down)
    grad_video, grads_one, biases_one, cond_one = backward_block(
        grad_middle, kept_one, first_back, cond_act, False
    )
    bias_sums = lax.psum(
        (
            jnp.stack([biases_one[0], biases_two[0]]),
            jnp.stack([biases_one[1], biases_two[1]]),
            jnp.stack([biases_one[2], biases_two[2]]),
            jnp.stack([biases_one[3], biases_two[3]]),
            jnp.stack([biases_one[4], biases_two[4]]),
        ),
        ("shard", "ctx"),
    )
    grad_act_total = lax.psum(cond_one + cond_two, ("ctx", "tp"))
    grad_cond = silu_back(grad_act_total)[0]
    return (
        result.astype(jnp.bfloat16),
        grad_video,
        grad_cond,
        jnp.stack([grads_one[0], grads_two[0]]),
        bias_sums[0],
        jnp.stack([grads_one[1], grads_two[1]]),
        bias_sums[1],
        jnp.stack([grads_one[2], grads_two[2]]),
        bias_sums[2],
        jnp.stack([grads_one[3], grads_two[3]]),
        bias_sums[3],
        jnp.stack([grads_one[4], grads_two[4]]),
        bias_sums[4],
    )


def solution(mesh):
    in_specs = (
        P("shard", "ctx", "tp", None, None),
        P("shard", None),
        P(None, "shard", "tp"),
        P(None, "tp"),
        P(None, None, "shard", "tp"),
        P(None, None, "tp"),
        P(None, "tp", "shard"),
        P(),
        P(None, "shard", "tp"),
        P(None, "tp"),
        P(None, "tp", "shard"),
        P(),
        P("shard", None, "tp", "ctx", None),
    )
    out_specs = (
        P("shard", None, "tp", "ctx", None),
        P("shard", "ctx", "tp", None, None),
        P("shard", None),
        P(None, "shard", "tp"),
        P(None, "tp"),
        P(None, None, "shard", "tp"),
        P(None, None, "tp"),
        P(None, "tp", "shard"),
        P(),
        P(None, "shard", "tp"),
        P(None, "tp"),
        P(None, "tp", "shard"),
        P(),
    )
    return jax.shard_map(body, mesh=mesh, in_specs=in_specs, out_specs=out_specs, check_vma=False)
```

profile of v0, /device:TPU:0, one launch (start us, length us, event | category | flops | bytes accessed | tf_op | source)
XLA Modules:
  0.0 2567.8 jit_solution(18138175500458335088)
XLA Ops:
  20.1 50.5 %all-gather.40.cloned.1.call-done = bf16[1,1152,1728]{2,1,0:T(8,128)(2,1)} async-done(((bf16[1,576,1728]{2,1,0:T(8,128)(2,1)}), bf16[1,1152,1728]{2,1,0:T(8,128)(2,1)}) %all-gather.40.cloned.1.call-update) | async-done | bytes 3981328 | tf_op jit(solution)/shard_map/all_gather | solution.py:96
  73.6 55.1 %all-gather.52.cloned.1.call-done = bf16[1,1152,1728]{2,1,0:T(8,128)(2,1)} async-done(((bf16[1,576,1728]{2,1,0:T(8,128)(2,1)}), bf16[1,1152,1728]{2,1,0:T(8,128)(2,1)}) %all-gather.52.cloned.1.call-update) | async-done | bytes 3981328 | tf_op jit(solution)/shard_map/all_gather | solution.py:96
  208.3 42.8 %all-gather.42.cloned.1.call-done = bf16[4,4,4,16,1152]{4,3,2,1,0:T(8,128)(2,1)} async-done(((bf16[1,4,4,16,1152]{4,3,2,1,0:T(8,128)(2,1)}), bf16[4,4,4,16,1152]{4,3,2,1,0:T(8,128)(2,1)}) %all-gather.42.cloned.1.call-update) | async-done | bytes 2359312 | tf_op jit(solution)/shard_map/all_gather | solution.py:115
  289.5 80.0 %reduce-scatter.33.cloned.1.call-done = f32[256,1152]{1,0:T(8,128)} async-done(((f32[1024,1152]{1,0:T(8,128)}), f32[256,1152]{1,0:T(8,128)}) %reduce-scatter.33.cloned.1.call-update) | async-done | bytes 1179664 | tf_op jit(solution)/shard_map/reduce_scatter | solution.py:123
  411.5 52.2 %all-gather.46.cloned.1.call-done = bf16[4,4,4,16,1152]{4,3,2,1,0:T(8,128)(2,1)} async-done(((bf16[1,4,4,16,1152]{4,3,2,1,0:T(8,128)(2,1)}), bf16[4,4,4,16,1152]{4,3,2,1,0:T(8,128)(2,1)}) %all-gather.46.cloned.1.call-update) | async-done | bytes 2359312 | tf_op jit(solution)/shard_map/all_gather | solution.py:115
  518.3 80.6 %reduce-scatter.35.cloned.1.call-done = f32[256,1152]{1,0:T(8,128)} async-done(((f32[1024,1152]{1,0:T(8,128)}), f32[256,1152]{1,0:T(8,128)}) %reduce-scatter.35.cloned.1.call-update) | async-done | bytes 1179664 | tf_op jit(solution)/shard_map/reduce_scatter | solution.py:123
  628.0 41.5 %all-gather.11 = bf16[1,288,1152]{1,0,2:T(2,128)(2,1)S(1)} all-gather(bf16[1,288,576]{1,0,2:T(2,128)(2,1)} %copy.344), channel_id=13, replica_groups=mesh['shard'=2,'ctx'=4,'tp'=4] {'shard'}, dimensions={2}, use_global_device_ids=true | all-gather | bytes 995328 | tf_op jit(solution)/shard_map/all_gather | solution.py:98
  680.3 41.6 %all-gather.34.cloned.1.call-done = bf16[4,1,16,4,4,1152]{5,2,4,3,1,0:T(8,128)(2,1)} async-done(((bf16[1,1,16,4,4,1152]{5,2,4,3,1,0:T(8,128)(2,1)}), bf16[4,1,16,4,4,1152]{5,2,4,3,1,0:T(8,128)(2,1)}) %all-gather.34.cloned.1.call-update) | async-done | bytes 2359312 | tf_op jit(solution)/shard_map/all_gather | solution.py:115
  763.2 84.2 %reduce-scatter.37.cloned.1.call-done = f32[256,1152]{1,0:T(8,128)} async-done(((f32[1024,1152]{1,0:T(8,128)}), f32[256,1152]{1,0:T(8,128)}) %reduce-scatter.37.cloned.1.call-update) | async-done | bytes 1179664 | tf_op jit(solution)/shard_map/reduce_scatter | solution.py:123
  866.7 47.4 %all-gather.36.cloned.1.call-done = bf16[4,1,16,4,4,1152]{5,2,4,3,1,0:T(8,128)(2,1)} async-done(((bf16[1,1,16,4,4,1152]{5,2,4,3,1,0:T(8,128)(2,1)}), bf16[4,1,16,4,4,1152]{5,2,4,3,1,0:T(8,128)(2,1)}) %all-gather.36.cloned.1.call-update) | async-done | bytes 2359312 | tf_op jit(solution)/shard_map/all_gather | solution.py:115
  1004.0 42.4 %all-gather.60.cloned.1.call-done = bf16[4,16,4,4,1152]{4,1,3,2,0:T(8,128)(2,1)} async-done(((bf16[1,16,4,4,1152]{4,1,3,2,0:T(8,128)(2,1)}), bf16[4,16,4,4,1152]{4,1,3,2,0:T(8,128)(2,1)}) %all-gather.60.cloned.1.call-update) | async-done | bytes 2359312 | tf_op jit(solution)/shard_map/all_gather | solution.py:119
  1079.1 53.6 %reduce-scatter.39.cloned.1.call-done = f32[256,1152]{1,0:T(8,128)} async-done(((f32[1024,1152]{1,0:T(8,128)}), f32[256,1152]{1,0:T(8,128)}) %reduce-scatter.39.cloned.1.call-update) | async-done | bytes 1179664 | tf_op jit(solution)/shard_map/reduce_scatter | solution.py:123
  1137.6 83.6 %reduce-scatter.41.cloned.1.call-done = f32[256,1152]{1,0:T(8,128)} async-done(((f32[1024,1152]{1,0:T(8,128)}), f32[256,1152]{1,0:T(8,128)}) %reduce-scatter.41.cloned.1.call-update) | async-done | bytes 1179664 | tf_op jit(solution)/shard_map/reduce_scatter | solution.py:129
  1241.0 49.7 %all-gather.62.cloned.1.call-done = bf16[4,16,4,4,1152]{4,1,3,2,0:T(8,128)(2,1)} async-done(((bf16[1,16,4,4,1152]{4,1,3,2,0:T(8,128)(2,1)}), bf16[4,16,4,4,1152]{4,1,3,2,0:T(8,128)(2,1)}) %all-gather.62.cloned.1.call-update) | async-done | bytes 2359312 | tf_op jit(solution)/shard_map/all_gather | solution.py:119
  1338.0 82.7 %reduce-scatter.43.cloned.1.call-done = f32[256,1152]{1,0:T(8,128)} async-done(((f32[1024,1152]{1,0:T(8,128)}), f32[256,1152]{1,0:T(8,128)}) %reduce-scatter.43.cloned.1.call-update) | async-done | bytes 1179664 | tf_op jit(solution)/shard_map/reduce_scatter | solution.py:129
  1453.4 49.7 %all-gather.38.cloned.1.call-done = bf16[4,1,4,4,16,1152]{5,4,3,2,1,0:T(8,128)(2,1)} async-done(((bf16[1,1,4,4,16,1152]{5,4,3,2,1,0:T(8,128)(2,1)}), bf16[4,1,4,4,16,1152]{5,4,3,2,1,0:T(8,128)(2,1)}) %all-gather.38.cloned.1.call-update) | async-done | bytes 2359312 | tf_op jit(solution)/shard_map/all_gather | solution.py:119
  1520.9 82.7 %reduce-scatter.45.cloned.1.call-done = f32[256,1152]{1,0:T(8,128)} async-done(((f32[1024,1152]{1,0:T(8,128)}), f32[256,1152]{1,0:T(8,128)}) %reduce-scatter.45.cloned.1.call-update) | async-done | bytes 1179664 | tf_op jit(solution)/shard_map/reduce_scatter | solution.py:129
  1611.2 50.6 %all-gather.64.cloned.1.call-done = bf16[4,4,4,16,1152]{4,3,2,1,0:T(8,128)(2,1)} async-done(((bf16[1,4,4,16,1152]{4,3,2,1,0:T(8,128)(2,1)}), bf16[4,4,4,16,1152]{4,3,2,1,0:T(8,128)(2,1)}) %all-gather.64.cloned.1.call-update) | async-done | bytes 2359312 | tf_op jit(solution)/shard_map/all_gather | solution.py:119
  1719.6 77.2 %reduce-scatter.47.cloned.1.call-done = f32[256,1152]{1,0:T(8,128)} async-done(((f32[1024,1152]{1,0:T(8,128)}), f32[256,1152]{1,0:T(8,128)}) %reduce-scatter.47.cloned.1.call-update) | async-done | bytes 1179664 | tf_op jit(solution)/shard_map/reduce_scatter | solution.py:129
  1886.4 49.3 %reduce-scatter.61.cloned.1.call-done = f32[1728,1]{1,0:T(8,128)} async-done(((f32[6912,1]{1,0:T(8,128)}), f32[1728,1]{1,0:T(8,128)}) %reduce-scatter.61.cloned.1.call-update) | async-done | bytes 6928 | tf_op jit(solution)/shard_map/reshape.135
  2166.9 40.9 %reduce-scatter.53.cloned.1.call-done = bf16[576,1152]{1,0:T(8,128)(2,1)} async-done(((bf16[1152,1152]{1,0:T(8,128)(2,1)}), bf16[576,1152]{1,0:T(8,128)(2,1)}) %reduce-scatter.53.cloned.1.call-update) | async-done | bytes 1327120 | tf_op jit(solution)/shard_map/reduce_scatter | solution.py:145
  2207.8 56.6 %reduce-scatter.49.cloned.1.call-done = bf16[576,1728]{1,0:T(8,128)(2,1)} async-done(((bf16[1152,1728]{1,0:T(8,128)(2,1)}), bf16[576,1728]{1,0:T(8,128)(2,1)}) %reduce-scatter.49.cloned.1.call-update) | async-done | bytes 1990672 | tf_op jit(solution)/shard_map/reduce_scatter | solution.py:136
  2264.4 56.4 %reduce-scatter.51.cloned.1.call-done = bf16[576,1728]{1,0:T(8,128)(2,1)} async-done(((bf16[1152,1728]{1,0:T(8,128)(2,1)}), bf16[576,1728]{1,0:T(8,128)(2,1)}) %reduce-scatter.51.cloned.1.call-update) | async-done | bytes 1990672 | tf_op jit(solution)/shard_map/reduce_scatter | solution.py:136
  2408.9 135.4 %all-reduce.7.cloned.1.call-done = (bf16[1,576,1728]{2,1,0:T(8,128)(2,1)}, bf16[1,576,1728]{2,1,0:T(8,128)(2,1)}, bf16[1,3,576,288]{2,3,1,0:T(8,128)(2,1)}, bf16...) async-done(((bf16[1,576,1728]{2,1,0:T(8,128)(2,1)}, ...) | async-done | bytes 11943952 | tf_op jit(solution)/shard_map/psum | solution.py:153
  (668 shorter events, 1063.8 us)
Async XLA Ops:
  12.5 188.8 %all-gather.44.cloned.1.call-start = ((), (), s32[]{:S(2)}) async-start(), calls=%async_computation.41 | async-start | bytes 5308416 | tf_op jit(solution)/shard_map/all_gather | solution.py:97
  17.4 233.7 %all-gather.42.cloned.1.call-start = ((), (), s32[]{:S(2)}) async-start(), calls=%async_computation.40 | async-start | bytes 2949120 | tf_op jit(solution)/shard_map/all_gather | solution.py:115
  153.8 215.7 %reduce-scatter.33.cloned.1.call-start = ((), (), s32[]{:S(2)}) async-start(), calls=%async_computation.22 | async-start | bytes 5898240 | tf_op jit(solution)/shard_map/reduce_scatter | solution.py:123
  288.9 174.8 %all-gather.46.cloned.1.call-start = ((), (), s32[]{:S(2)}) async-start(), calls=%async_computation.42 | async-start | bytes 2949120 | tf_op jit(solution)/shard_map/all_gather | solution.py:115
  376.8 222.1 %reduce-scatter.35.cloned.1.call-start = ((), (), s32[]{:S(2)}) async-start(), calls=%async_computation.23 | async-start | bytes 5898240 | tf_op jit(solution)/shard_map/reduce_scatter | solution.py:123
  624.7 222.7 %reduce-scatter.37.cloned.1.call-start = ((), (), s32[]{:S(2)}) async-start(), calls=%async_computation.25 | async-start | bytes 5898240 | tf_op jit(solution)/shard_map/reduce_scatter | solution.py:123
  864.6 181.9 %all-gather.60.cloned.1.call-start = ((), (), s32[]{:S(2)}) async-start(), calls=%async_computation.49 | async-start | bytes 2949120 | tf_op jit(solution)/shard_map/all_gather | solution.py:119
  866.7 266.0 %reduce-scatter.39.cloned.1.call-start = ((), (), s32[]{:S(2)}) async-start(), calls=%async_computation.27 | async-start | bytes 5898240 | tf_op jit(solution)/shard_map/reduce_scatter | solution.py:123
  1004.0 217.3 %reduce-scatter.41.cloned.1.call-start = ((), (), s32[]{:S(2)}) async-start(), calls=%async_computation.28 | async-start | bytes 5898240 | tf_op jit(solution)/shard_map/reduce_scatter | solution.py:129
  1071.2 219.5 %all-gather.62.cloned.1.call-start = ((), (), s32[]{:S(2)}) async-start(), calls=%async_computation.50 | async-start | bytes 2949120 | tf_op jit(solution)/shard_map/all_gather | solution.py:119
  1240.0 180.7 %reduce-scatter.43.cloned.1.call-start = ((), (), s32[]{:S(2)}) async-start(), calls=%async_computation.29 | async-start | bytes 5898240 | tf_op jit(solution)/shard_map/reduce_scatter | solution.py:129
  1611.1 185.7 %reduce-scatter.47.cloned.1.call-start = ((), (), s32[]{:S(2)}) async-start(), calls=%async_computation.32 | async-start | bytes 5898240 | tf_op jit(solution)/shard_map/reduce_scatter | solution.py:129
  1712.6 172.3 %reduce-scatter.63.cloned.1.call-start = ((), (), s32[]{:S(2)}) async-start(), calls=%async_computation.53 | async-start | bytes 4423680 | tf_op jit(solution)/shard_map/reshape.137
  1715.7 219.9 %reduce-scatter.61.cloned.1.call-start = ((), (), s32[]{:S(2)}) async-start(), calls=%async_computation.52 | async-start | bytes 4423680 | tf_op jit(solution)/shard_map/reshape.135
  1807.3 183.6 %reduce-scatter.67.cloned.1.call-start = ((), (), s32[]{:S(2)}) async-start(), calls=%async_computation.55 | async-start | bytes 3096576
  1827.9 183.9 %reduce-scatter.69.cloned.1.call-start = ((), (), s32[]{:S(2)}) async-start(), calls=%async_computation.56 | async-start | bytes 1327104
  1832.9 212.6 %reduce-scatter.65.cloned.1.call-start = ((), (), s32[]{:S(2)}) async-start(), calls=%async_computation.54 | async-start | bytes 3096576
  1853.5 233.0 %reduce-scatter.55.cloned.1.call-start = ((), (), s32[]{:S(2)}) async-start(), calls=%async_computation.36 | async-start | bytes 3981312 | tf_op jit(solution)/shard_map/reduce_scatter | solution.py:145
  1860.7 266.0 %reduce-scatter.59.cloned.1.call-start = ((), (), s32[]{:S(2)}) async-start(), calls=%async_computation.38 | async-start | bytes 3981312 | tf_op jit(solution)/shard_map/reduce_scatter | solution.py:148
  1868.8 298.1 %reduce-scatter.57.cloned.1.call-start = ((), (), s32[]{:S(2)}) async-start(), calls=%async_computation.37 | async-start | bytes 3981312 | tf_op jit(solution)/shard_map/reduce_scatter | solution.py:148
  1877.0 330.8 %reduce-scatter.53.cloned.1.call-start = ((), (), s32[]{:S(2)}) async-start(), calls=%async_computation.35 | async-start | bytes 3981312 | tf_op jit(solution)/shard_map/reduce_scatter | solution.py:145
  1884.2 380.2 %reduce-scatter.49.cloned.1.call-start = ((), (), s32[]{:S(2)}) async-start(), calls=%async_computation.33 | async-start | bytes 6193152 | tf_op jit(solution)/shard_map/reduce_scatter | solution.py:136
  1943.2 377.6 %reduce-scatter.51.cloned.1.call-start = ((), (), s32[]{:S(2)}) async-start(), calls=%async_computation.34 | async-start | bytes 6193152 | tf_op jit(solution)/shard_map/reduce_scatter | solution.py:136
  1943.8 600.5 %all-reduce.7.cloned.1.call-start = ((), (), s32[]{:S(2)}) async-start(), calls=%async_computation.58 | async-start | bytes 24772608 | tf_op jit(solution)/shard_map/psum | solution.py:153
  (151 other events, 4353.8 us)
Sparse Core Ops, SparseCore 0:
  11.8 58.6 all-gather.39
  72.7 55.9 all-gather.51
  130.8 68.2 all-gather.43
  201.2 49.9 all-gather.41
  285.5 84.0 reduce-scatter.32
  413.6 49.9 all-gather.45
  513.6 85.2 reduce-scatter.34
  600.9 68.7 all-gather.53
  671.8 50.0 all-gather.33
  763.3 84.0 reduce-scatter.36
  863.6 50.5 all-gather.35
  996.5 49.9 all-gather.59
  1048.6 84.0 reduce-scatter.38
  1135.4 85.7 reduce-scatter.40
  1240.2 50.4 all-gather.61
  1336.6 84.0 reduce-scatter.42
  1519.5 84.0 reduce-scatter.44
  1611.2 50.4 all-gather.63
  1712.7 84.0 reduce-scatter.46
  1799.1 67.0 reduce-scatter.62
  1868.9 66.6 reduce-scatter.60
  2210.7 53.6 reduce-scatter.48
  2267.1 53.6 reduce-scatter.50
  2324.8 219.4 all-reduce.6
  (13 shorter events, 456.8 us)
where the time goes:
time: 2580 us; the launch traced here: 2570 us
  waiting for transfers between devices  1790 us (69%)
  local copies, waits for them, and re-layouts  290 us (11%)
  matrix products  183 us (7%)
  blocking collectives  174 us (7%)
  other arithmetic  106 us (4%)
    reduce_scatter x4, waiting for transfers between devices, reduce_grads(): lax.psum_scatter(term(jnp.int32(0), own_rows * lax.axis_size('tp')), 'tp'...  326 us
    reduce_scatter x4, waiting for transfers between devices, reduce_rows(): lax.psum_scatter(term(jnp.int32(0), own_rows * lax.axis_size('tp')), 'tp'...  298 us
    all_gather x4, waiting for transfers between devices, spread_grads(): return lax.all_gather(values[None], 'tp', axis=0, tiled=True)  192 us
    all_gather x4, waiting for transfers between devices, spread_rows(): return lax.all_gather(values[None], 'tp', axis=0, tiled=True)  184 us
    psum x1, waiting for transfers between devices, sum_weight_grads(): lax.psum(summed[0].astype(jnp.bfloat16), 'ctx').astype(jnp.float32)  135 us
    reduce_scatter x2, waiting for transfers between devices, sum_weight_grads(): lax.psum_scatter(grads[0].astype(jnp.bfloat16), 'shard', scatter_dimensio...  113 us
    all_gather x2, waiting for transfers between devices, fetch_forward(): lax.all_gather(w_ada[number], 'shard', axis=0, tiled=True)  106 us
    unnamed x41, waiting for transfers between devices  93.9 us
  transfers between devices with their start and end apart: 38, of which 35 were waited for; matrix products, arithmetic and copies ran while one was open for 11% of the time, Pallas kernels for 0%

commit v1 on v0

v1 whole, which is shorter than its diff:
```python
from functools import partial
import math

import jax
import jax.numpy as jnp
from jax import lax
from jax.experimental import pallas as pl
from jax.experimental.pallas import tpu as pltpu
from jax.sharding import PartitionSpec as P

HEAD_DIM = 72
GROUP = 256

bf16 = jnp.bfloat16
f32 = jnp.float32
highest = lax.Precision.HIGHEST


def layer_norm(values):
    average = jnp.mean(values, axis=-1, keepdims=True)
    centered = values - average
    spread = jnp.mean(centered * centered, axis=-1, keepdims=True)
    return centered * lax.rsqrt(spread + 1e-06)


def modulate(values, offset, factor):
    return layer_norm(values) * (1.0 + factor) + offset


def dot_nt(left, right):
    return lax.dot_general(left, right, (((1,), (1,)), ((), ())), preferred_element_type=f32)


def dot_nn(left, right):
    return lax.dot_general(left, right, (((1,), (0,)), ((), ())), preferred_element_type=f32)


def dot_tn(left, right):
    return lax.dot_general(left, right, (((0,), (0,)), ((), ())), preferred_element_type=f32)


def swap(values, axis, bit):
    count = lax.axis_size(axis)
    return lax.ppermute(values, axis, [(i, i ^ bit) for i in range(count)])


def bits_of(axis):
    count = lax.axis_size(axis)
    assert count & (count - 1) == 0
    found = []
    while count > 1:
        count //= 2
        found.append(count)
    return found


def spread(values, axis="ctx"):
    slots = {0: values}
    for bit in bits_of(axis):
        for key in list(slots):
            slots[key ^ bit] = swap(slots[key], axis, bit)
    return [slots[key] for key in range(len(slots))]


def collect(terms, axis="ctx"):
    slots = dict(enumerate(terms))
    for bit in reversed(bits_of(axis)):
        for key in sorted((k for k in slots if k & bit), reverse=True):
            sent = swap(slots.pop(key).astype(bf16), axis, bit)
            slots[key ^ bit] = slots[key ^ bit] + sent.astype(f32)
    return slots[0]


def sum_over(values, axis):
    for bit in reversed(bits_of(axis)):
        values = values + swap(values, axis, bit)
    return values


def shifted(values, axis, shift):
    count = lax.axis_size(axis)
    return lax.ppermute(values, axis, [(i, (i + shift) % count) for i in range(count)])


def small_gather(values, axis):
    count = lax.axis_size(axis)
    own = lax.axis_index(axis)
    parts = jnp.stack([values] + [shifted(values, axis, k) for k in range(1, count)])
    return jnp.take(parts, (own - jnp.arange(count)) % count, axis=0)


def small_exchange(values, axis):
    count = lax.axis_size(axis)
    own = lax.axis_index(axis)
    pick = lambda k: lax.dynamic_index_in_dim(values, (own + k) % count, 0, keepdims=False)
    return [pick(0)] + [shifted(pick(k), axis, k) for k in range(1, count)]


def small_scatter(values, axis):
    return sum(small_exchange(values, axis))


def small_all_to_all(values, axis):
    count = lax.axis_size(axis)
    own = lax.axis_index(axis)
    parts = jnp.stack(small_exchange(values, axis))
    return jnp.take(parts, (own - jnp.arange(count)) % count, axis=0)


def turn(values):
    count = lax.axis_size("ctx")
    assert count == lax.axis_size("tp")
    pairs = [(i * count + j, j * count + i) for i in range(count) for j in range(count)]
    return lax.ppermute(values, ("ctx", "tp"), pairs)


def group_mask(seen):
    row = lax.broadcasted_iota(jnp.int32, (GROUP, GROUP), 0)
    column = lax.broadcasted_iota(jnp.int32, (GROUP, GROUP), 1)
    return (row % seen) == (column % seen)


def probs_of(query, key, own_head, seen):
    scores = dot_nt(query * own_head, key) * (1.0 / math.sqrt(HEAD_DIM))
    if seen > 1:
        scores = jnp.where(group_mask(seen), scores, -1e30)
    weights = jnp.exp(scores - jnp.max(scores, axis=-1, keepdims=True))
    return weights * (1.0 / jnp.sum(weights, axis=-1, keepdims=True))


def attend_kernel(heads_ref, qkv_ref, out_ref, *, seen):
    cut = lambda n: qkv_ref[n].reshape(GROUP, qkv_ref.shape[-1])
    query, key, value = cut(0), cut(1), cut(2)
    total = None
    for head in range(heads_ref.shape[0]):
        own_head = heads_ref[head : head + 1, :]
        probs = probs_of(query, key, own_head, seen)
        part = dot_nn(probs.astype(bf16), value * own_head)
        total = part if total is None else total + part
    out_ref[...] = total.astype(bf16).reshape(out_ref.shape)


def attend_back_kernel(heads_ref, qkv_ref, grad_ref, out_ref, *, seen):
    cut = lambda n: qkv_ref[n].reshape(GROUP, qkv_ref.shape[-1])
    query, key, value = cut(0), cut(1), cut(2)
    grad = grad_ref[...].reshape(GROUP, grad_ref.shape[-1])
    factor = 1.0 / math.sqrt(HEAD_DIM)
    totals = [None, None, None]
    for head in range(heads_ref.shape[0]):
        own_head = heads_ref[head : head + 1, :]
        probs = probs_of(query, key, own_head, seen)
        own_grad = grad * own_head
        grad_value = dot_tn(probs.astype(bf16), own_grad)
        grad_probs = dot_nt(own_grad, value)
        inner = jnp.sum(grad_probs * probs, axis=-1, keepdims=True)
        grad_scores = (probs * (grad_probs - inner)).astype(bf16)
        grad_query = dot_nn(grad_scores, key * own_head)
        grad_key = dot_tn(grad_scores, query * own_head)
        parts = (grad_query, grad_key, grad_value)
        totals = [p if t is None else t + p for t, p in zip(totals, parts)]
    for number, scale in enumerate((factor, factor, 1.0)):
        result = (totals[number] * scale).astype(bf16)
        out_ref[number] = result.reshape(out_ref.shape[1:])


def head_masks(columns):
    head = jnp.arange(columns)[None, :] // HEAD_DIM
    return (head == jnp.arange(columns // HEAD_DIM)[:, None]).astype(bf16)


def group_specs(rows, columns, parts):
    slot = GROUP // parts
    groups = rows // GROUP
    shape = (parts, groups, slot, columns)
    block = (parts, 1, slot, columns)
    plain = pl.BlockSpec(block, lambda g: (0, g, 0, 0))
    stacked = pl.BlockSpec((3,) + block, lambda g: (0, 0, g, 0, 0))
    heads = pl.BlockSpec((columns // HEAD_DIM, columns), lambda g: (0, 0))
    return groups, shape, heads, plain, stacked


def attend(qkv, parts, seen):
    rows, columns = qkv.shape[1:]
    groups, shape, heads, plain, stacked = group_specs(rows, columns, parts)
    result = pl.pallas_call(
        partial(attend_kernel, seen=seen),
        grid=(groups,),
        in_specs=[heads, stacked],
        out_specs=plain,
        out_shape=jax.ShapeDtypeStruct(shape, bf16),
        name="attend",
    )(head_masks(columns), qkv.reshape((3,) + shape))
    return result.reshape(rows, columns)


def attend_back(qkv, grad, parts, seen):
    rows, columns = qkv.shape[1:]
    groups, shape, heads, plain, stacked = group_specs(rows, columns, parts)
    result = pl.pallas_call(
        partial(attend_back_kernel, seen=seen),
        grid=(groups,),
        in_specs=[heads, stacked, plain],
        out_specs=stacked,
        out_shape=jax.ShapeDtypeStruct((3,) + shape, bf16),
        name="attend_back",
    )(head_masks(columns), qkv.reshape((3,) + shape), grad.reshape(shape))
    return result.reshape(3, rows, columns)


def own_part(values, axis):
    count = lax.axis_size("ctx")
    split = values.shape[axis] // count
    return lax.dynamic_slice_in_dim(values, lax.axis_index("ctx") * split, split, axis)


def fetch(piece):
    shards, quarters = lax.axis_size("shard"), lax.axis_size("tp")
    units, columns = piece.shape
    whole = lax.all_gather(piece[None], ("shard", "tp"), axis=0, tiled=True)
    whole = whole.reshape(shards, quarters, units, columns)
    return jnp.transpose(whole, (1, 2, 0, 3))


def fetch_block(number, w_qkv, w_out, w_up, w_down):
    quarters = lax.axis_size("tp")
    width = w_out.shape[2] * lax.axis_size("shard")
    qkv = jnp.transpose(own_part(w_qkv[number], 2), (0, 2, 1))
    units = qkv.shape[1]
    attn = jnp.concatenate([qkv.reshape(3 * units, -1), own_part(w_out[number], 0)])
    attn = fetch(attn).reshape(quarters, 4, units, width)
    attn = jnp.transpose(attn, (1, 0, 2, 3)).reshape(4, quarters * units, width)
    up = fetch(jnp.transpose(own_part(w_up[number], 1))).reshape(-1, width)
    down = fetch(own_part(w_down[number], 0)).reshape(-1, width)
    return (attn[:3], attn[3], up, down)


def reduce_weights(grad):
    shards = lax.axis_size("shard")
    quarters, units, width = grad.shape
    pieces = grad.astype(bf16).reshape(quarters, units, shards, width // shards)
    pieces = jnp.transpose(pieces, (2, 0, 1, 3)).reshape(shards * quarters, units, -1)
    own = lax.psum_scatter(pieces, ("shard", "tp"), scatter_dimension=0, tiled=True)
    own = own.reshape(units, width // shards)
    slots = spread(own)
    order = jnp.arange(len(slots)) ^ lax.axis_index("ctx")
    return jnp.take(jnp.stack(slots), order, axis=0).astype(f32)


def forward_block(inputs, modulation, weights, b_qv, b_out, b_up, b_down, parts, seen):
    w_qkv, w_out, w_up, w_down = weights
    own_rows = inputs.shape[0]
    shift_a, scale_a, gate_a, shift_m, scale_m, gate_m = modulation
    hidden = jnp.concatenate(spread(modulate(inputs, shift_a, scale_a).astype(bf16)))
    projected = jnp.einsum("rd,tcd->trc", hidden, w_qkv, preferred_element_type=f32)
    bias = jnp.stack([b_qv[0], jnp.zeros_like(b_qv[0]), b_qv[1]])
    qkv = (projected + bias[:, None, :]).astype(bf16)
    attended = attend(qkv, parts, seen)
    attn_out = reduce_product(attended, w_out, own_rows) + b_out
    after_attn = inputs + gate_a * attn_out
    hidden_two = jnp.concatenate(spread(modulate(after_attn, shift_m, scale_m).astype(bf16)))
    up_rows = dot_nt(hidden_two, w_up) + b_up
    activated = jax.nn.gelu(up_rows, approximate=True).astype(bf16)
    mlp_out = reduce_product(activated, w_down, own_rows) + b_down
    result = after_attn + gate_m * mlp_out
    kept = (inputs, after_attn, hidden, qkv, attended, attn_out, hidden_two, up_rows, mlp_out)
    return (result, kept)


def reduce_product(left, right, own_rows):
    count = left.shape[0] // own_rows
    half = (count // 2) * own_rows
    far = dot_nn(left[half:], right)
    near = dot_nn(left[:half], right)
    cut = lambda rows: [rows[n : n + own_rows] for n in range(0, half, own_rows)]
    return collect(cut(near) + cut(far))


def backward_block(grad_y, kept, modulation, weights, parts, seen):
    inputs, after_attn, hidden, qkv, attended, attn_out, hidden_two, up_rows, mlp_out = kept
    w_qkv, w_out, w_up, w_down = weights
    own_rows = inputs.shape[0]
    quarters = lax.axis_size("tp")
    shift_a, scale_a, gate_a, shift_m, scale_m, gate_m = modulation
    token_sum = lambda values: jnp.sum(values, axis=0, keepdims=True, dtype=f32)

    grad_mlp = (gate_m * grad_y).astype(bf16)
    grad_rows = jnp.concatenate(spread(grad_mlp))
    grad_gate_m = token_sum(grad_y * mlp_out)
    grad_b_down = token_sum(grad_mlp)
    activated, gelu_back = jax.vjp(partial(jax.nn.gelu, approximate=True), up_rows)
    grad_up = gelu_back(dot_nt(grad_rows, w_down))[0].astype(bf16)
    grad_hidden_two = reduce_product(grad_up, w_up, own_rows)
    by_quarter = lambda grad: grad.reshape(quarters, -1, grad.shape[-1])
    grad_w_down = reduce_weights(by_quarter(dot_tn(activated.astype(bf16), grad_rows)))
    grad_w_up = reduce_weights(by_quarter(dot_tn(grad_up, hidden_two)))
    grad_b_up = token_sum(grad_up)
    unused_two, norm_back_two = jax.vjp(modulate, after_attn, shift_m, scale_m)
    grad_norm_two, grad_shift_m, grad_scale_m = norm_back_two(grad_hidden_two)
    grad_after = grad_y + grad_norm_two

    grad_attn = (gate_a * grad_after).astype(bf16)
    grad_rows = jnp.concatenate(spread(grad_attn))
    grad_gate_a = token_sum(grad_after * attn_out)
    grad_b_out = token_sum(grad_attn)
    grad_attended = dot_nt(grad_rows, w_out).astype(bf16)
    grad_qkv = attend_back(qkv, grad_attended, parts, seen)
    terms = [(grad_qkv[n], w_qkv[n]) for n in range(3)]
    half = grad_qkv.shape[1] // 2
    far = sum(dot_nn(left[half:], right) for left, right in terms)
    near = sum(dot_nn(left[:half], right) for left, right in terms)
    cut = lambda rows: [rows[n : n + own_rows] for n in range(0, half, own_rows)]
    grad_hidden = collect(cut(near) + cut(far))
    grad_w = [by_quarter(dot_tn(grad_qkv[n], hidden)) for n in range(3)]
    grad_w.append(by_quarter(dot_tn(attended, grad_rows)))
    grad_w_attn = reduce_weights(jnp.concatenate(grad_w, axis=1))
    grad_b_qv = jnp.stack([jnp.sum(grad_qkv[n], axis=0, dtype=f32) for n in (0, 2)])
    unused_one, norm_back_one = jax.vjp(modulate, inputs, shift_a, scale_a)
    grad_norm_one, grad_shift_a, grad_scale_a = norm_back_one(grad_hidden)
    grad_inputs = grad_after + grad_norm_one

    grad_mod = (grad_shift_a, grad_scale_a, grad_gate_a, grad_shift_m, grad_scale_m, grad_gate_m)
    small = sum_small(jnp.concatenate(grad_mod, axis=1), grad_b_qv, grad_b_up, grad_b_out, grad_b_down)
    return (grad_inputs, (grad_w_attn, grad_w_up, grad_w_down), small)


def sum_small(grad_mod, grad_b_qv, grad_b_up, grad_b_out, grad_b_down):
    quarters, members = lax.axis_size("tp"), lax.axis_size("ctx")
    own = lax.axis_index("ctx")

    def placed(values):
        count = values.shape[0]
        values = jnp.transpose(values.reshape(count, quarters, 1, -1), (1, 0, 2, 3))
        slots = (jnp.arange(members) == own).astype(f32)[None, None, :, None]
        return (values * slots).reshape(quarters, -1)

    quarter = lambda values: values.reshape(quarters, -1)
    pieces = [
        quarter(grad_mod),
        placed(grad_b_up),
        placed(grad_b_qv),
        quarter(grad_b_out),
        quarter(grad_b_down),
    ]
    sizes = [piece.shape[1] for piece in pieces]
    packed = small_scatter(jnp.concatenate(pieces, axis=1), "tp")
    packed = small_gather(sum_over(packed, "ctx"), "shard")
    edges = [sum(sizes[:n]) for n in range(len(sizes) + 1)]
    parts = [packed[:, edges[n] : edges[n + 1]] for n in range(len(sizes))]
    totals = [jnp.sum(part, axis=0) for part in parts]
    ends = small_gather(jnp.stack(totals[3:]), "tp")
    return (
        parts[0],
        totals[0],
        totals[1],
        totals[2].reshape(2, -1),
        ends[:, 0].reshape(-1),
        ends[:, 1].reshape(-1),
    )


def body(
    video, cond, w_ada, b_ada, w_qkv, b_qv, w_out, b_out, w_up, b_up, w_down, b_down, cotangent
):
    clips, own_frames, own_lines, columns, width = video.shape
    assert clips == 1
    quarters = lax.axis_size("tp")
    own_t = lax.axis_index("ctx")

    cond_act, silu_back = jax.vjp(jax.nn.silu, cond.astype(f32))
    cond_all = small_gather(cond_act.astype(bf16)[0], "shard")
    shard_rows = w_ada.shape[1]
    cond_rows = lax.dynamic_slice_in_dim(
        cond_all, lax.axis_index("shard") * shard_rows, shard_rows, 1
    )
    mod_terms = jnp.einsum("sd,bdm->sbm", cond_rows, w_ada, preferred_element_type=f32)
    mod_part = small_scatter(mod_terms, "shard") + b_ada
    modulation = small_gather(mod_part, "tp")
    modulation = jnp.transpose(modulation, (1, 0, 2)).reshape(2, 6, 1, width)
    mods = [[modulation[b, n] for n in range(6)] for b in range(2)]

    moved = lax.all_to_all(turn(video), "ctx", split_axis=3, concat_axis=2, tiled=True)
    spatial_shape = moved.shape
    temporal_shape = cotangent.shape

    first = fetch_block(0, w_qkv, w_out, w_up, w_down)
    second = fetch_block(1, w_qkv, w_out, w_up, w_down)

    def member_bias(bias, units):
        whole = small_gather(bias, "tp")
        members = whole.reshape(whole.shape[:-1] + (-1, units))
        own = lax.dynamic_index_in_dim(members, own_t, members.ndim - 2, keepdims=False)
        return jnp.moveaxis(own, 0, -2).reshape(bias.shape[:-1] + (-1,)).astype(f32)

    members = lax.axis_size("ctx")
    up_bias = member_bias(b_up, b_up.shape[-1] // members)
    qv_bias = member_bias(b_qv, b_qv.shape[-1] // members)

    rows = lambda values: values.reshape(-1, width)
    spatial = (members, 1)
    frames = temporal_shape[1]
    temporal = (1, GROUP // frames)
    middle, kept_one = forward_block(
        rows(moved).astype(f32), mods[0], first, qv_bias[0], b_out[0], up_bias[0], b_down[0], *spatial
    )
    middle = lax.all_to_all(
        middle.astype(bf16).reshape(spatial_shape), "tp", split_axis=2, concat_axis=1, tiled=True
    )
    result, kept_two = forward_block(
        rows(middle).astype(f32), mods[1], second, qv_bias[1], b_out[1], up_bias[1], b_down[1], *temporal
    )
    grad_moved, weights_two, small_two = backward_block(
        rows(cotangent).astype(f32), kept_two, mods[1], second, *temporal
    )
    grad_middle = lax.all_to_all(
        grad_moved.astype(bf16).reshape(temporal_shape), "tp", split_axis=1, concat_axis=2, tiled=True
    )
    grad_first, weights_one, small_one = backward_block(
        rows(grad_middle).astype(f32), kept_one, mods[0], first, *spatial
    )
    grad_video = lax.all_to_all(
        grad_first.astype(bf16).reshape(spatial_shape), "ctx", split_axis=2, concat_axis=3, tiled=True
    )
    grad_video = turn(grad_video).astype(f32)

    small = (small_one, small_two)
    cond_float = cond_rows.astype(f32)
    grad_w_ada = jnp.stack(
        [
            sum(
                cond_float[s][:, None] * small[b][0][s][None, :]
                for s in range(cond_float.shape[0])
            )
            for b in range(2)
        ]
    )
    grad_cond = sum(
        jnp.dot(small[b][0], w_ada[b].astype(f32).T, precision=highest) for b in range(2)
    )
    grad_cond = small_all_to_all(sum_over(grad_cond, "tp"), "shard").reshape(1, -1)
    grad_cond = silu_back(grad_cond)[0]

    both = (weights_one, weights_two)
    attn = jnp.stack([grads[0] for grads in both])
    up = jnp.stack([grads[1] for grads in both])
    down = jnp.stack([grads[2] for grads in both])
    attn = attn.reshape(2, members, 4, attn.shape[2] // 4, shard_rows)
    grad_w_qkv = jnp.transpose(attn[:, :, :3], (0, 2, 4, 1, 3)).reshape(w_qkv.shape)
    grad_w_out = attn[:, :, 3].reshape(w_out.shape)
    grad_w_up = jnp.transpose(up, (0, 3, 1, 2)).reshape(w_up.shape)
    grad_w_down = down.reshape(w_down.shape)
    stacked = [jnp.stack([small[b][n] for b in range(2)]) for n in range(1, 6)]
    return (
        result.astype(bf16).reshape(temporal_shape),
        grad_video,
        grad_cond,
        grad_w_ada,
        stacked[0],
        grad_w_qkv,
        stacked[2],
        grad_w_out,
        stacked[3],
        grad_w_up,
        stacked[1],
        grad_w_down,
        stacked[4],
    )


def solution(mesh):
    in_specs = (
        P("shard", "ctx", "tp", None, None),
        P("shard", None),
        P(None, "shard", "tp"),
        P(None, "tp"),
        P(None, None, "shard", "tp"),
        P(None, None, "tp"),
        P(None, "tp", "shard"),
        P(),
        P(None, "shard", "tp"),
        P(None, "tp"),
        P(None, "tp", "shard"),
        P(),
        P("shard", None, "tp", "ctx", None),
    )
    out_specs = (
        P("shard", None, "tp", "ctx", None),
        P("shard", "ctx", "tp", None, None),
        P("shard", None),
        P(None, "shard", "tp"),
        P(None, "tp"),
        P(None, None, "shard", "tp"),
        P(None, None, "tp"),
        P(None, "tp", "shard"),
        P(),
        P(None, "shard", "tp"),
        P(None, "tp"),
        P(None, "tp", "shard"),
        P(),
    )
    return jax.shard_map(body, mesh=mesh, in_specs=in_specs, out_specs=out_specs, check_vma=False)
```

time: 2580 us -> 1030 us (0.40)
  waiting for transfers between devices: 1790 us -> 323 us
  blocking collectives: 174 us -> 23.3 us
  starting transfers between devices: 6.16 us -> 89.8 us
  matrix products: 183 us -> 134 us
  Pallas kernels: 0 us -> 43 us
    reduce_scatter x14 -> x6, waiting for transfers between devices: 893 us -> 82.1 us  [reduce_weights(): lax.psum_scatter(pieces, ('shard', 'tp'), scatter_dimension=0, tiled=True)]
    all_gather x16 -> x6, waiting for transfers between devices: 611 us -> 30.6 us  [fetch(): whole = lax.all_gather(piece[None], ('shard', 'tp'), axis=0, tiled=True)]
    ppermute x0 -> x100, waiting for transfers between devices: none -> 196 us  [the longest x72 154 us: swap(): return lax.ppermute(values, axis, [(i, i ^ bit) for i in range(count)])]
    psum x1 -> x0, waiting for transfers between devices: 135 us -> none  [sum_weight_grads(): lax.psum(summed[0].astype(jnp.bfloat16), 'ctx').astype(jnp.float32)]
    unnamed x41 -> x12, waiting for transfers between devices: 93.9 us -> 0.2 us
    all_gather x2 -> x0, blocking collectives: 82.2 us -> none  [fetch_forward(): lax.all_gather(w_out[number], 'shard', axis=1, tiled=True)]
    ppermute x0 -> x100, starting transfers between devices: none -> 78.3 us  [the longest x72 38.1 us: swap(): return lax.ppermute(values, axis, [(i, i ^ bit) for i in range(count)])]
    psum x2 -> x0, blocking collectives: 59.7 us -> none  [the longest x1 33.9 us: body(): grad_act_total = lax.psum(cond_one + cond_two, ('ctx', 'tp'))]
  transfers between devices with their start and end apart: 38 -> 115, of which waited for: 35 -> 39; matrix products, arithmetic and copies ran while one was open for 11% -> 42% of each run, Pallas kernels for 0% -> 4%
where the time goes in v1:
time: 1030 us; the launch traced here: 1020 us
  waiting for transfers between devices  323 us (31%)
  local copies, waits for them, and re-layouts  288 us (28%)
  matrix products  134 us (13%)
  other arithmetic  101 us (10%)
  starting transfers between devices  89.8 us (9%)
  Pallas kernels  43 us (4%)
  blocking collectives  23.3 us (2%)
  between operations  17.6 us (2%)
    ppermute x72, waiting for transfers between devices, swap(): return lax.ppermute(values, axis, [(i, i ^ bit) for i in range(count)])  154 us
    reduce_scatter x6, waiting for transfers between devices, reduce_weights(): lax.psum_scatter(pieces, ('shard', 'tp'), scatter_dimension=0, tiled=True)  82.1 us
    dot_general x12, matrix products, dot_tn(): lax.dot_general(left, right, (((0,), (0,)), ((), ())), preferred_element_...  43.7 us
    ppermute x26, waiting for transfers between devices, shifted(): lax.ppermute(values, axis, [(i, (i + shift) % count) for i in range(count)])  42.1 us
    dot_general x6, matrix products, dot_nt(): lax.dot_general(left, right, (((1,), (1,)), ((), ())), preferred_element_...  41.6 us
    convert_element_type x8, local copies, waits for them, and re-layouts, reduce_weights(): pieces = grad.astype(bf16).reshape(quarters, units, shards, width // shards)  39.1 us
    unnamed x446, local copies, waits for them, and re-layouts  38.2 us
    ppermute x72, starting transfers between devices, swap(): return lax.ppermute(values, axis, [(i, i ^ bit) for i in range(count)])  38.1 us
  transfers between devices with their start and end apart: 115, of which 39 were waited for; matrix products, arithmetic and copies ran while one was open for 42% of the time, Pallas kernels for 4%

profile of v1, /device:TPU:0, one launch (start us, length us, event | category | flops | bytes accessed | tf_op | source)
XLA Modules:
  0.0 1020.4 jit_solution(15639928270203503226)
XLA Ops:
  45.0 21.5 %collective-permute-done.4 = f32[2,1728]{1,0:T(2,128)S(1)} collective-permute-done((f32[2,1728]{1,0:T(2,128)S(1)}, f32[2,1728]{1,0:T(2,128)S(1)}, u32[]{:S(2)}, u32[]{:S(2)}) %collective-permute-start.4) | collective-permute-done | bytes 13856 | tf_op jit(solution)/shard_map/ppermute | solution.py:82
  72.8 8.4 all-to-all-done
  125.8 8.8 attend.2
  146.8 12.7 %collective-permute-done.14 = bf16[256,1152]{1,0:T(8,128)(2,1)S(1)} collective-permute-done((bf16[256,1152]{1,0:T(8,128)(2,1)}, bf16[256,1152]{1,0:T(8,128)(2,1)S(1)}, u32[]{:S(2)}, u32[]{:S(2)}) %collective-permute-start.14) | collective-permute-done | bytes 589856 | tf_op jit(solution)/shard_map/ppermute | solution.py:44
  163.0 14.0 %collective-permute-done.16 = bf16[256,1152]{1,0:T(8,128)(2,1)S(1)} collective-permute-done((bf16[256,1152]{1,0:T(8,128)(2,1)S(1)}, bf16[256,1152]{1,0:T(8,128)(2,1)S(1)}, u32[]{:S(2)}, u32[]{:S(2)}) %collective-permute-start.16) | collective-permute-done | bytes 589856 | tf_op jit(solution)/shard_map/ppermute | solution.py:44
  200.2 11.2 %all-gather.11.cloned.1.call-done = bf16[8,288,576]{2,1,0:T(8,128)(2,1)} async-done(((bf16[1,288,576]{2,1,0:T(8,128)(2,1)}), bf16[8,288,576]{2,1,0:T(8,128)(2,1)}) %all-gather.11.cloned.1.call-update) | async-done | bytes 2654224 | tf_op jit(solution)/shard_map/all_gather | solution.py:219
  224.7 8.2 multiply_convert_fusion.1
  244.6 13.2 %collective-permute-done.23 = bf16[256,1152]{1,0:T(8,128)(2,1)S(1)} collective-permute-done((bf16[256,1152]{1,0:T(8,128)(2,1)S(1)}, bf16[256,1152]{1,0:T(8,128)(2,1)S(1)}, u32[]{:S(2)}, u32[]{:S(2)}) %collective-permute-start.23) | collective-permute-done | bytes 589856 | tf_op jit(solution)/shard_map/ppermute | solution.py:44
  259.3 23.3 %all_to_all.45 = bf16[1,4,16,4,1152]{4,3,1,0,2:T(4,128)(2,1)S(1)} all-to-all(bf16[1,4,16,4,1152]{4,3,1,0,2:T(4,128)(2,1)S(1)} %copy.187), channel_id=1, replica_groups=mesh['shard'=2,'ctx'=4,'tp'=4] {'tp'}, dimensions={2} | all-to-all | bytes 1179648 | tf_op jit(solution)/shard_map/all_to_all | solution.py:405
  317.5 8.8 attend.3
  331.5 14.4 %collective-permute-done.29 = bf16[256,1152]{1,0:T(8,128)(2,1)S(1)} collective-permute-done((bf16[256,1152]{1,0:T(8,128)(2,1)S(1)}, bf16[256,1152]{1,0:T(8,128)(2,1)S(1)}, u32[]{:S(2)}, u32[]{:S(2)}) %collective-permute-start.29) | collective-permute-done | bytes 589856 | tf_op jit(solution)/shard_map/ppermute | solution.py:44
  348.1 14.0 %collective-permute-done.31 = bf16[256,1152]{1,0:T(8,128)(2,1)} collective-permute-done((bf16[256,1152]{1,0:T(8,128)(2,1)S(1)}, bf16[256,1152]{1,0:T(8,128)(2,1)}, u32[]{:S(2)}, u32[]{:S(2)}) %collective-permute-start.31) | collective-permute-done | bytes 589856 | tf_op jit(solution)/shard_map/ppermute | solution.py:44
  375.7 19.4 %all-gather.13.cloned.1.call-done = bf16[8,288,576]{2,1,0:T(8,128)(2,1)} async-done(((bf16[1,288,576]{2,1,0:T(8,128)(2,1)}), bf16[8,288,576]{2,1,0:T(8,128)(2,1)}) %all-gather.13.cloned.1.call-update) | async-done | bytes 2654224 | tf_op jit(solution)/shard_map/all_gather | solution.py:219
  408.3 8.4 multiply_convert_fusion
  425.9 12.7 %collective-permute-done.35 = bf16[256,1152]{1,0:T(8,128)(2,1)} collective-permute-done((bf16[256,1152]{1,0:T(8,128)(2,1)}, bf16[256,1152]{1,0:T(8,128)(2,1)}, u32[]{:S(2)}, u32[]{:S(2)}) %collective-permute-start.35) | collective-permute-done | bytes 589856 | tf_op jit(solution)/shard_map/ppermute | solution.py:44
  443.7 12.9 %collective-permute-done.37 = bf16[256,1152]{1,0:T(8,128)(2,1)S(1)} collective-permute-done((bf16[256,1152]{1,0:T(8,128)(2,1)S(1)}, bf16[256,1152]{1,0:T(8,128)(2,1)S(1)}, u32[]{:S(2)}, u32[]{:S(2)}) %collective-permute-start.37) | collective-permute-done | bytes 589856 | tf_op jit(solution)/shard_map/ppermute | solution.py:44
  464.3 7.4 convert_element_type.498
  475.6 10.3 %convert_reduce_fusion = (f32[1152]{0:T(1024)}, bf16[1024,1152]{1,0:T(8,128)(2,1)S(1)}) fusion(f32[1024,1152]{1,0:T(8,128)} %get-tuple-element.228, bf16[1152,1152]{1,0:T(8,128)(2,1)} %reshape.975, bf16[256,1152]{1,0:T(8,128)(2,1)} %copy-done.208, bf16[256,1152]{1,0:T(8,128)(2,1)} %copy-done.206, bf16[256,1152]{1,0:T(8,128)(2,1)} %copy-done.207, ...), kind=kOutput, calls=%fused_computation.38 | convolution fusion | flops 2753297408 | bytes 12096000 | tf_op jit(solution)/shard_map/dot_general | solution.py:31
  493.2 12.7 %collective-permute-done.41 = bf16[256,1152]{1,0:T(8,128)(2,1)S(1)} collective-permute-done((bf16[256,1152]{1,0:T(8,128)(2,1)S(1)}, bf16[256,1152]{1,0:T(8,128)(2,1)S(1)}, u32[]{:S(2)}, u32[]{:S(2)}) %collective-permute-start.41) | collective-permute-done | bytes 589856 | tf_op jit(solution)/shard_map/ppermute | solution.py:44
  531.9 7.5 convert_element_type.494
  550.0 12.7 %attend_back.2 = bf16[3,1,4,256,288]{4,3,2,1,0:T(8,128)(2,1)} custom-call(bf16[4,288]{1,0:T(4,128)(2,1)} %fusion.80.heads_ref, bf16[3,1,4,256,288]{4,3,2,1,0:T(8,128)(2,1)} %bitcast.412, bf16[1,4,256,288]{3,2,1,0:T(8,128)(2,1)} %bitcast.467), custom_call_target="tpu_custom_call" | custom-call | tf_op jit(solution)/shard_map/attend_back/pallas_call | solution.py:199
  677.1 9.1 convert_reduce_fusion.1
  748.2 12.7 %attend_back.3 = bf16[3,4,4,64,288]{4,3,2,1,0:T(8,128)(2,1)} custom-call(bf16[4,288]{1,0:T(4,128)(2,1)} %fusion.80.heads_ref, bf16[3,4,4,64,288]{4,3,2,1,0:T(8,128)(2,1)} %bitcast.410, bf16[4,4,64,288]{3,2,1,0:T(8,128)(2,1)} %bitcast.466), custom_call_target="tpu_custom_call" | custom-call | tf_op jit(solution)/shard_map/attend_back/pallas_call | solution.py:199
  878.5 82.1 %reduce-scatter.7.cloned.1.call-done = bf16[1,288,576]{2,1,0:T(8,128)(2,1)} async-done(((bf16[8,288,576]{2,1,0:T(8,128)(2,1)}), bf16[1,288,576]{2,1,0:T(8,128)(2,1)}) %reduce-scatter.7.cloned.1.call-update) | async-done | bytes 331792 | tf_op jit(solution)/shard_map/reduce_scatter | solution.py:242
  (1045 shorter events, 636.6 us)
Async XLA Ops:
  7.2 96.3 %all-gather.15.cloned.1.call-start = ((), (), s32[]{:S(2)}) async-start(), calls=%async_computation.18 | async-start | bytes 3317760 | tf_op jit(solution)/shard_map/all_gather | solution.py:219
  15.0 171.9 %all-gather.17.cloned.1.call-start = ((), (), s32[]{:S(2)}) async-start(), calls=%async_computation.19 | async-start | bytes 3317760 | tf_op jit(solution)/shard_map/all_gather | solution.py:219
  17.5 193.9 %all-gather.11.cloned.1.call-start = ((), (), s32[]{:S(2)}) async-start(), calls=%async_computation.10 | async-start | bytes 3317760 | tf_op jit(solution)/shard_map/all_gather | solution.py:219
  21.1 46.0 %collective-permute-start = (bf16[1,4,4,16,1152]{4,3,2,1,0:T(8,128)(2,1)}, bf16[1,4,4,16,1152]{4,3,2,1,0:T(8,128)(2,1)S(1)}, u32[]{:S(2)}, u32[]{:S(2)}) collective-permute-start(bf16[1,4,4,16,1152]{4,3,2,1,0:T(8,128)(2,1)} %param.19), channel_id=1, source_target_pairs={{0,0},{1,4},{2,8},{3,12},{4,1},{5,5},{6,9},{7,13},{8,2},{9,6},{10,... | collective-permute-start | bytes 1769480 | tf_op jit(solution)/shard_map/ppermute | solution.py:114
  71.7 216.8 %all-gather.19.cloned.1.call-start = ((), (), s32[]{:S(2)}) async-start(), calls=%async_computation.20 | async-start | bytes 3317760 | tf_op jit(solution)/shard_map/all_gather | solution.py:219
  146.2 216.0 %all-gather.21.cloned.1.call-start = ((), (), s32[]{:S(2)}) async-start(), calls=%async_computation.21 | async-start | bytes 3317760 | tf_op jit(solution)/shard_map/all_gather | solution.py:219
  163.0 61.6 %collective-permute-start.15 = (bf16[256,1152]{1,0:T(8,128)(2,1)S(1)}, bf16[256,1152]{1,0:T(8,128)(2,1)}, u32[]{:S(2)}, u32[]{:S(2)}) collective-permute-start(bf16[256,1152]{1,0:T(8,128)(2,1)S(1)} %add_convert_fusion.8), channel_id=1, source_target_pairs={{0,4},{4,0},{8,12},{12,8},{1,5},{5,1},{9,13},{13,9},{2,6},{6,2},{1... | collective-permute-start | bytes 1769480 | tf_op jit(solution)/shard_map/ppermute | solution.py:44
  177.0 47.6 %collective-permute-start.17 = (bf16[256,1152]{1,0:T(8,128)(2,1)S(1)}, bf16[256,1152]{1,0:T(8,128)(2,1)}, u32[]{:S(2)}, u32[]{:S(2)}) collective-permute-start(bf16[256,1152]{1,0:T(8,128)(2,1)S(1)} %collective-permute-done.16), channel_id=1, source_target_pairs={{0,4},{4,0},{8,12},{12,8},{1,5},{5,1},{9,13},{13,9},{2,6},{6,2},{1... | collective-permute-start | bytes 1769480 | tf_op jit(solution)/shard_map/ppermute | solution.py:44
  237.3 157.8 %all-gather.13.cloned.1.call-start = ((), (), s32[]{:S(2)}) async-start(), calls=%async_computation.11 | async-start | bytes 3317760 | tf_op jit(solution)/shard_map/all_gather | solution.py:219
  288.4 410.4 %reduce-scatter.17.cloned.1.call-start = ((), (), s32[]{:S(2)}) async-start(), calls=%async_computation.17 | async-start | bytes 3317760 | tf_op jit(solution)/shard_map/reduce_scatter | solution.py:242
  348.1 60.2 %collective-permute-start.30 = (bf16[256,1152]{1,0:T(8,128)(2,1)S(1)}, bf16[256,1152]{1,0:T(8,128)(2,1)}, u32[]{:S(2)}, u32[]{:S(2)}) collective-permute-start(bf16[256,1152]{1,0:T(8,128)(2,1)S(1)} %add_convert_fusion.5), channel_id=1, source_target_pairs={{0,4},{4,0},{8,12},{12,8},{1,5},{5,1},{9,13},{13,9},{2,6},{6,2},{1... | collective-permute-start | bytes 1769480 | tf_op jit(solution)/shard_map/ppermute | solution.py:44
  362.1 46.2 %collective-permute-start.32 = (bf16[256,1152]{1,0:T(8,128)(2,1)}, bf16[256,1152]{1,0:T(8,128)(2,1)}, u32[]{:S(2)}, u32[]{:S(2)}) collective-permute-start(bf16[256,1152]{1,0:T(8,128)(2,1)} %collective-permute-done.31), channel_id=1, source_target_pairs={{0,4},{4,0},{8,12},{12,8},{1,5},{5,1},{9,13},{13,9},{2,6},{6,2},{1... | collective-permute-start | bytes 1769480 | tf_op jit(solution)/shard_map/ppermute | solution.py:44
  475.5 224.8 %reduce-scatter.13.cloned.1.call-start = ((), (), s32[]{:S(2)}) async-start(), calls=%async_computation.15 | async-start | bytes 3317760 | tf_op jit(solution)/shard_map/reduce_scatter | solution.py:242
  543.3 249.0 %reduce-scatter.9.cloned.1.call-start = ((), (), s32[]{:S(2)}) async-start(), calls=%async_computation.13 | async-start | bytes 3317760 | tf_op jit(solution)/shard_map/reduce_scatter | solution.py:242
  615.9 257.7 %reduce-scatter.15.cloned.1.call-start = ((), (), s32[]{:S(2)}) async-start(), calls=%async_computation.16 | async-start | bytes 3317760 | tf_op jit(solution)/shard_map/reduce_scatter | solution.py:242
  675.3 202.8 %reduce-scatter.11.cloned.1.call-start = ((), (), s32[]{:S(2)}) async-start(), calls=%async_computation.14 | async-start | bytes 3317760 | tf_op jit(solution)/shard_map/reduce_scatter | solution.py:242
  698.8 32.4 %collective-permute-start.98 = (bf16[288,576]{1,0:T(8,128)(2,1)}, bf16[288,576]{1,0:T(8,128)(2,1)}, u32[]{:S(2)}, u32[]{:S(2)}) collective-permute-start(bf16[288,576]{1,0:T(8,128)(2,1)} %bitcast.521), channel_id=1, source_target_pairs={{0,8},{4,12},{8,0},{12,4},{1,9},{5,13},{9,1},{13,5},{2,10},{6,14},... | collective-permute-start | bytes 995336 | tf_op jit(solution)/shard_map/ppermute | solution.py:44
  700.9 39.3 %collective-permute-start.91 = (bf16[288,576]{1,0:T(8,128)(2,1)}, bf16[288,576]{1,0:T(8,128)(2,1)}, u32[]{:S(2)}, u32[]{:S(2)}) collective-permute-start(bf16[288,576]{1,0:T(8,128)(2,1)} %bitcast.524), channel_id=1, source_target_pairs={{0,4},{4,0},{8,12},{12,8},{1,5},{5,1},{9,13},{13,9},{2,6},{6,2},{1... | collective-permute-start | bytes 995336 | tf_op jit(solution)/shard_map/ppermute | solution.py:44
  730.7 229.8 %reduce-scatter.7.cloned.1.call-start = ((), (), s32[]{:S(2)}) async-start(), calls=%async_computation.12 | async-start | bytes 3317760 | tf_op jit(solution)/shard_map/reduce_scatter | solution.py:242
  832.7 36.0 %all-to-all-start.3 = ((bf16[1,4,16,4,1152]{4,3,1,0,2:T(4,128)(2,1)}), bf16[1,4,16,4,1152]{4,3,1,0,2:T(4,128)(2,1)S(1)}, u32[]{:S(2)}, u32[]{:S(2)}) async-start(bf16[1,4,16,4,1152]{4,3,1,0,2:T(4,128)(2,1)} %copy.200), calls=%async_computation.3 | async-start | bytes 1179648 | tf_op jit(solution)/shard_map/all_to_all | solution.py:420
  869.1 93.8 %collective-permute-start.60 = (bf16[1,4,4,16,1152]{4,3,2,1,0:T(8,128)(2,1)S(1)}, bf16[1,4,4,16,1152]{4,3,2,1,0:T(8,128)(2,1)S(1)}, u32[]{:S(2)}, u32[]{:S(2)}) collective-permute-start(bf16[1,4,4,16,1152]{4,3,2,1,0:T(8,128)(2,1)S(1)} %all_to_all.40), channel_id=1, source_target_pairs={{0,0},{1,4},{2,8},{3,12},{4,1},{5,5},{6,9},{7,13},{8,2},{9,6},{10,... | collective-permute-start | bytes 1769480 | tf_op jit(solution)/shard_map/ppermute | solution.py:114
  873.5 89.4 %collective-permute-start.95 = (bf16[288,576]{1,0:T(8,128)(2,1)}, bf16[288,576]{1,0:T(8,128)(2,1)S(1)}, u32[]{:S(2)}, u32[]{:S(2)}) collective-permute-start(bf16[288,576]{1,0:T(8,128)(2,1)} %bitcast.515), channel_id=1, source_target_pairs={{0,8},{4,12},{8,0},{12,4},{1,9},{5,13},{9,1},{13,5},{2,10},{6,14},... | collective-permute-start | bytes 995336 | tf_op jit(solution)/shard_map/ppermute | solution.py:44
  877.2 86.3 %collective-permute-start.94 = (bf16[288,576]{1,0:T(8,128)(2,1)}, bf16[288,576]{1,0:T(8,128)(2,1)S(1)}, u32[]{:S(2)}, u32[]{:S(2)}) collective-permute-start(bf16[288,576]{1,0:T(8,128)(2,1)} %bitcast.516), channel_id=1, source_target_pairs={{0,4},{4,0},{8,12},{12,8},{1,5},{5,1},{9,13},{13,9},{2,6},{6,2},{1... | collective-permute-start | bytes 995336 | tf_op jit(solution)/shard_map/ppermute | solution.py:44
  878.2 85.3 %collective-permute-start.89 = (bf16[288,576]{1,0:T(8,128)(2,1)}, bf16[288,576]{1,0:T(8,128)(2,1)S(1)}, u32[]{:S(2)}, u32[]{:S(2)}) collective-permute-start(bf16[288,576]{1,0:T(8,128)(2,1)} %bitcast.519), channel_id=1, source_target_pairs={{0,8},{4,12},{8,0},{12,4},{1,9},{5,13},{9,1},{13,5},{2,10},{6,14},... | collective-permute-start | bytes 995336 | tf_op jit(solution)/shard_map/ppermute | solution.py:44
  (306 other events, 3145.1 us)
Sparse Core Ops, SparseCore 0:
  15.2 78.7 all-gather.14
  96.1 56.4 all-gather.16
  154.7 56.5 all-gather.10
  213.3 63.9 all-gather.18
  279.8 56.0 all-gather.20
  338.5 56.5 all-gather.12
  475.6 71.7 reduce-scatter.16
  551.5 77.4 reduce-scatter.12
  633.1 71.7 reduce-scatter.8
  708.9 73.5 reduce-scatter.14
  786.7 73.5 reduce-scatter.10
  864.3 96.2 reduce-scatter.6
